TPU v7x, 512 devices: a whole 4x4x16 slice. The times are simulated.
512 devices in a mesh: seq: 64 (over y, z), mp: 8 (over x, core).
Axes of the slice: x: 4, y: 4, z: 16, core: 2. Of those that a mesh axis runs over, the one named last changes fastest.
Arguments:
- byte_states: bfloat16 [16384, 1024], P('seq'), may hold values from -6 to 6
- outer_gain: float32 [1024], replicated, may hold values from 0.1 to 1.9
- mamba_input: bfloat16 [1024, 1024], P(None, 'mp'), may hold values from -0.1875 to 0.1875
- mamba_step: bfloat16 [1024, 1024], P(None, 'mp'), may hold values from -0.1875 to 0.1875
- decay_rate: float32 [1024], P('mp'), as said below
- mixer_weight: bfloat16 [1024, 1024], P('mp'), may hold values from -0.1875 to 0.1875
- boundaries: int32 [64, 128], P('seq'), may hold values from 0 to 256, as said below
- span_counts: int32 [64], replicated, may hold values from 1 to 128, as said below
- up_weight: bfloat16 [1024, 4096], P('seq', 'mp'), may hold values from -0.1875 to 0.1875
- up_bias: float32 [4096], P('mp'), may hold values from -5 to 5
- inner_gain: float32 [4096], replicated, as said below
- query_weight: bfloat16 [4096, 4096], P('seq', 'mp'), as said below
- key_weight: bfloat16 [4096, 1024], P('seq', 'mp'), as said below
- value_weight: bfloat16 [4096, 1024], P('seq', 'mp'), may hold values from -0.09375 to 0.09375
- return_weight: bfloat16 [4096, 1024], P('mp'), may hold values from -0.09375 to 0.09375
Outputs:
- joined: bfloat16 [16384, 1024], P('seq', 'mp')
Inputs may be any that keep to these rules, and one draw needn't show every extreme that they name: `boundaries`: row s lists the spans of shard s: its first span_counts[s] entries rise strictly from 0 and are byte positions within the shard; each span runs to the next entry, the last to the shard's end; the other entries equal 256. `span_counts`: the counts sum to 4096; some shard has exactly 128 spans. `decay_rate`: Positive. `inner_gain`: Positive. `query_weight`: Finite. `key_weight`: Finite.
All inputs are finite; a program needn't handle non-finite values.
Results may differ from a plain program's by a relative error of at most 0.01.
Values may be sent and summed in bfloat16 or wider, within the bound.
A program may use at most 64 MiB of HBM per device.

v0:
```python
import math
import jax
import jax.numpy as jnp
from jax import lax
from jax.sharding import PartitionSpec as P

HEADS = 32
KV_HEADS = 8
HEAD = 128
eps = 1e-05
masked = -1e30
far_index = 1073741824


def prefix(value, axis, join, neutral):
    count, mine = (lax.axis_size(axis), lax.axis_index(axis))
    pieces = jax.tree.map(lambda part: lax.all_gather(part, axis), value)
    so_far = jax.tree.map(
        lambda part, zero: jnp.full_like(part, 0) + jnp.asarray(zero, part.dtype), value, neutral
    )

    def lap(position, so_far):
        longer = join(so_far, jax.tree.map(lambda part: part[position], pieces))
        return jax.tree.map(lambda new, old: jnp.where(position < mine, new, old), longer, so_far)

    return lax.fori_loop(0, count - 1, lap, so_far)


def rms_scale(values, gain):
    values = values.astype(jnp.float32)
    return values * lax.rsqrt(jnp.mean(values * values, axis=-1, keepdims=True) + eps) * gain


def combine_pairs(earlier, later):
    return (earlier[0] * later[0], later[0] * earlier[1] + later[1])


def pick_table(table, wanted, seq_ids):
    return jnp.sum(jnp.where(seq_ids[None, :] == wanted[:, None], table[None, :], 0), axis=1)


def block_size(piece_rows, shard_rows):
    limit = max(1, 1024 // shard_rows)
    pieces = max(1, piece_rows // shard_rows)
    best_size = 1
    for candidate in range(1, limit + 1):
        if pieces % candidate == 0:
            best_size = candidate
    return min(piece_rows, best_size * shard_rows)


def on_device(
    byte_states,
    outer_gain,
    mamba_input,
    mamba_step,
    decay_rate,
    mixer_weight,
    boundaries,
    span_counts,
    up_weight,
    up_bias,
    inner_gain,
    query_weight,
    key_weight,
    value_weight,
    return_weight,
):
    shards = lax.axis_size("seq")
    own_shard = lax.axis_index("seq")
    own_lane = lax.axis_index("mp")
    rows_here = byte_states.shape[0]
    capacity = boundaries.shape[1]
    column_count = mamba_input.shape[1]
    kv_local = key_weight.shape[1] // HEAD
    group_size = HEADS // KV_HEADS
    offsets = jnp.cumsum(span_counts) - span_counts
    seq_ids = jnp.arange(shards, dtype=jnp.int32)
    own_offset = jnp.sum(jnp.where(seq_ids == own_shard, offsets, 0))
    own_count = jnp.sum(jnp.where(seq_ids == own_shard, span_counts, 0))
    normed = rms_scale(byte_states, outer_gain).astype(jnp.bfloat16)
    inputs = jnp.dot(normed, mamba_input, preferred_element_type=jnp.float32)
    step_sizes = jax.nn.softplus(jnp.dot(normed, mamba_step, preferred_element_type=jnp.float32))
    rate_steps = step_sizes * decay_rate
    decays = jnp.exp(-rate_steps)
    drives = jnp.sqrt(-jnp.expm1(-2.0 * rate_steps)) * inputs
    through, local_states = lax.associative_scan(combine_pairs, (decays, drives), axis=0)
    starting = (jnp.ones((column_count,), jnp.float32), jnp.zeros((column_count,), jnp.float32))
    arriving = prefix((through[-1], local_states[-1]), "seq", combine_pairs, starting)
    states = (local_states + through * arriving[1][None, :]).astype(jnp.bfloat16)
    partial_value = jnp.dot(states, mixer_weight, preferred_element_type=jnp.float32)
    mixed_sum = lax.psum(partial_value, "mp")
    encoded = (byte_states.astype(jnp.float32) + mixed_sum).astype(jnp.bfloat16)
    skip_part = lax.dynamic_slice_in_dim(encoded, own_lane * column_count, column_count, 1)
    own_marks = boundaries[0]
    pooled = encoded[jnp.minimum(own_marks, rows_here - 1)]
    local_slot = jnp.arange(capacity, dtype=jnp.int32)
    query_index = jnp.where(local_slot < own_count, own_offset + local_slot, -1)
    columns = pooled
    widened_sum = jnp.dot(
        columns,
        lax.all_gather(up_weight, "seq", axis=0, tiled=True),
        preferred_element_type=jnp.float32,
    )
    widened_share = (widened_sum + up_bias[None, :]).astype(jnp.bfloat16)
    widened = lax.all_gather(widened_share, "mp", axis=1, tiled=True)
    inner_normed = rms_scale(widened, inner_gain).astype(jnp.bfloat16)
    columns = inner_normed
    query_part = jnp.dot(
        columns,
        lax.all_gather(query_weight, "seq", axis=0, tiled=True),
        preferred_element_type=jnp.float32,
    )
    key_part = jnp.dot(
        columns,
        lax.all_gather(key_weight, "seq", axis=0, tiled=True),
        preferred_element_type=jnp.float32,
    )
    value_part = jnp.dot(
        columns,
        lax.all_gather(value_weight, "seq", axis=0, tiled=True),
        preferred_element_type=jnp.float32,
    )
    queries = query_part.astype(jnp.bfloat16)
    key_rows = key_part.astype(jnp.bfloat16)
    value_rows = value_part.astype(jnp.bfloat16)
    query_count = queries.shape[0]
    grouped = (
        queries.reshape(query_count, kv_local, group_size, HEAD)
        .transpose(1, 0, 2, 3)
        .reshape(kv_local, query_count * group_size, HEAD)
    )
    row_index = jnp.repeat(query_index, group_size)
    shard_rows = key_rows.shape[0]
    score_scale = 1.0 / math.sqrt(HEAD)

    def key_index(whole_index):
        holder = whole_index // shard_rows
        within = whole_index % shard_rows
        holder_offset = pick_table(offsets, holder, seq_ids)
        holder_count = pick_table(span_counts, holder, seq_ids)
        return jnp.where(within < holder_count, holder_offset + within, far_index)

    def attend_block(running, key_block, value_block, index_block):
        row_peak, denominator, weighted = running
        scores = (
            jnp.einsum("hqd,khd->hqk", grouped, key_block, preferred_element_type=jnp.float32)
            * score_scale
        )
        scores = jnp.where(index_block[None, None, :] <= row_index[None, :, None], scores, masked)
        new_peak = jnp.maximum(row_peak, jnp.max(scores, axis=2))
        shrink = jnp.exp(row_peak - new_peak)
        lifted = jnp.exp(scores - new_peak[:, :, None])
        denominator = denominator * shrink + jnp.sum(lifted, axis=2)
        weighted = weighted * shrink[:, :, None] + jnp.einsum(
            "hqk,khd->hqd",
            lifted.astype(jnp.bfloat16),
            value_block,
            preferred_element_type=jnp.float32,
        )
        return (new_peak, denominator, weighted)

    query_total = query_count * group_size
    initial = (
        jnp.full((kv_local, query_total), masked, jnp.float32),
        jnp.zeros((kv_local, query_total), jnp.float32),
        jnp.zeros((kv_local, query_total, HEAD), jnp.float32),
    )
    key_piece = lax.all_gather(key_rows, "seq", axis=0, tiled=True)
    value_piece = lax.all_gather(value_rows, "seq", axis=0, tiled=True)
    piece_rows = key_piece.shape[0]
    block_rows = block_size(piece_rows, shard_rows)
    turn_count = piece_rows // block_rows
    key_blocks = key_piece.reshape(turn_count, block_rows, kv_local, HEAD)
    value_blocks = value_piece.reshape(turn_count, block_rows, kv_local, HEAD)

    def one_turn(turn_index, inner_running):
        whole_index = turn_index * block_rows + jnp.arange(block_rows, dtype=jnp.int32)
        return attend_block(
            inner_running, key_blocks[turn_index], value_blocks[turn_index], key_index(whole_index)
        )

    row_peak, denominator, weighted = lax.fori_loop(0, turn_count, one_turn, initial)
    attended = (weighted / denominator[:, :, None]).astype(jnp.bfloat16)
    attended = (
        attended.reshape(kv_local, query_count, group_size, HEAD)
        .transpose(1, 0, 2, 3)
        .reshape(query_count, kv_local * group_size * HEAD)
    )
    projected = jnp.dot(attended, return_weight, preferred_element_type=jnp.float32)
    returned = lax.psum_scatter(
        projected.astype(jnp.bfloat16), "mp", scatter_dimension=1, tiled=True
    )
    positions = jnp.arange(rows_here, dtype=jnp.int32)
    live_slots = jnp.arange(capacity, dtype=jnp.int32) < own_count
    passed = jnp.sum(
        ((own_marks[None, :] <= positions[:, None]) & live_slots[None, :]).astype(jnp.int32), axis=1
    )
    return (skip_part.astype(jnp.float32) + returned[passed - 1].astype(jnp.float32)).astype(
        jnp.bfloat16
    )


def solution(mesh):
    in_specs = (
        P("seq", None),
        P(),
        P(None, "mp"),
        P(None, "mp"),
        P("mp"),
        P("mp", None),
        P("seq", None),
        P(),
        P("seq", "mp"),
        P("mp"),
        P(),
        P("seq", "mp"),
        P("seq", "mp"),
        P("seq", "mp"),
        P("mp", None),
    )
    out_specs = P("seq", "mp")
    return jax.shard_map(
        on_device, mesh=mesh, in_specs=in_specs, out_specs=out_specs, check_vma=False
    )
```

profile of v0, /device:TPU:8, one launch (start us, length us, event | category | flops | bytes accessed | tf_op | source)
XLA Modules:
  0.0 1139.2 jit_solution(18261109659851616036)
XLA Ops:
  8.8 1.5 negate_exponential_fusion
  12.6 79.6 %all-gather.1 = f32[64,1,128]{2,1,0:T(1,128)S(1)} all-gather(f32[1,1,128]{2,1,0:T(1,128)S(1)} %add_bitcast_fusion), channel_id=1, replica_groups=mesh['seq'=64,'mp'=8] {'seq'}, dimensions={0}, use_global_device_ids=true | all-gather | bytes 33280 | tf_op jit(solution)/shard_map/all_gather | solution.py:17
  92.3 73.3 %all-gather = f32[64,1,128]{2,1,0:T(1,128)S(1)} all-gather(f32[1,1,128]{2,1,0:T(1,128)S(1)} %add_bitcast_fusion.1), channel_id=1, replica_groups=mesh['seq'=64,'mp'=8] {'seq'}, dimensions={0}, use_global_device_ids=true | all-gather | bytes 33280 | tf_op jit(solution)/shard_map/all_gather | solution.py:17
  165.6 2.6 while.34
  170.2 73.0 %all-reduce.34.cloned.1.call-done = f32[256,1024]{1,0:T(8,128)} async-done(((f32[256,1024]{1,0:T(8,128)}), f32[256,1024]{1,0:T(8,128)}) %all-reduce.34.cloned.1.call-update) | async-done | bytes 1048592 | tf_op jit(solution)/shard_map/psum | solution.py:92
  245.5 61.3 %all-gather.10.cloned.1.call-done = bf16[1024,512]{1,0:T(8,128)(2,1)} async-done(((bf16[16,512]{1,0:T(8,128)(2,1)}), bf16[1024,512]{1,0:T(8,128)(2,1)}) %all-gather.10.cloned.1.call-update) | async-done | bytes 1048592 | tf_op jit(solution)/shard_map/all_gather | solution.py:102
  306.7 2.2 fusion.31
  310.9 26.2 %all-gather.12.cloned.1.call-done = bf16[128,4096]{1,0:T(8,128)(2,1)} async-done(((bf16[128,512]{1,0:T(8,128)(2,1)}), bf16[128,4096]{1,0:T(8,128)(2,1)}) %all-gather.12.cloned.1.call-update) | async-done | bytes 1048592 | tf_op jit(solution)/shard_map/all_gather | solution.py:106
  337.1 1.6 fusion.28
  338.8 140.2 %all-gather.20.cloned.1.call-done = bf16[4096,128]{1,0:T(8,128)(2,1)} async-done(((bf16[64,128]{1,0:T(8,128)(2,1)}), bf16[4096,128]{1,0:T(8,128)(2,1)}) %all-gather.20.cloned.1.call-update) | async-done | bytes 1048592 | tf_op jit(solution)/shard_map/all_gather | solution.py:121
  478.9 2.7 convolution_convert_fusion.2
  481.7 136.0 %all-gather.14.cloned.1.call-done = bf16[4096,128]{1,0:T(8,128)(2,1)} async-done(((bf16[64,128]{1,0:T(8,128)(2,1)}), bf16[4096,128]{1,0:T(8,128)(2,1)}) %all-gather.14.cloned.1.call-update) | async-done | bytes 1048592 | tf_op jit(solution)/shard_map/all_gather | solution.py:116
  617.7 2.3 convolution_convert_fusion.3
  622.5 1.9 add_select_fusion.3
  625.1 137.2 %all-gather.18.cloned.1.call-done = bf16[4096,512]{1,0:T(8,128)(2,1)} async-done(((bf16[64,512]{1,0:T(8,128)(2,1)}), bf16[4096,512]{1,0:T(8,128)(2,1)}) %all-gather.18.cloned.1.call-update) | async-done | bytes 4194320 | tf_op jit(solution)/shard_map/all_gather | solution.py:111
  762.2 3.0 convolution_convert_fusion.1
  765.3 135.9 %all-gather.22.cloned.1.call-done = bf16[8192,128]{1,0:T(8,128)(2,1)} async-done(((bf16[128,128]{1,0:T(8,128)(2,1)}), bf16[8192,128]{1,0:T(8,128)(2,1)}) %all-gather.22.cloned.1.call-update) | async-done | bytes 2097168 | tf_op jit(solution)/shard_map/all_gather | solution.py:170
  901.2 140.0 %all-gather.16.cloned.1.call-done = bf16[8192,128]{1,0:T(8,128)(2,1)} async-done(((bf16[128,128]{1,0:T(8,128)(2,1)}), bf16[8192,128]{1,0:T(8,128)(2,1)}) %all-gather.16.cloned.1.call-update) | async-done | bytes 2097168 | tf_op jit(solution)/shard_map/all_gather | solution.py:169
  1041.2 50.0 %while.35 = (s32[]{:T(128)}, f32[1,512]{1,0:T(1,128)S(1)}, f32[1,512]{1,0:T(1,128)S(1)}, f32[1,512,128]{2,1,0:T(8,128)S(1)}, s32[64]{0:T(128)S(1)}, /*index=5*/s...) while((s32[]{:T(128)}, f32[1,512]{1,0:T(1,128)S(1)}, ...), condition=%wide.region_13.14_spmd.clone, body=%wide.region_8.13_spmd.clone.sunk | while | flops 273186304 | bytes 7548097 | solution.py:183
  1042.9 2.0 fusion.78
  1049.2 2.0 fusion.78
  1055.4 2.0 fusion.78
  1058.5 1.5 fusion.82
  1061.7 2.0 fusion.78
  1064.7 1.5 fusion.82
  1067.9 2.0 fusion.78
  1071.0 1.5 fusion.82
  1074.1 2.0 fusion.78
  1080.4 2.0 fusion.78
  1086.6 2.0 fusion.78
  1092.7 35.8 %reduce-scatter.4.cloned.1.call-done = bf16[128,128]{1,0:T(8,128)(2,1)} async-done(((bf16[1024,128]{1,0:T(8,128)(2,1)}), bf16[128,128]{1,0:T(8,128)(2,1)}) %reduce-scatter.4.cloned.1.call-update) | async-done | bytes 32784
  1130.3 1.5 add_convert_fusion
  (351 shorter events, 45.8 us)
Async XLA Ops:
  7.4 1084.1 %copy-start = (bf16[512,1024]{1,0:T(8,128)(2,1)S(1)}, bf16[512,1024]{1,0:T(8,128)(2,1)}, u32[]{:S(2)}) copy-start(bf16[512,1024]{1,0:T(8,128)(2,1)} %param.33) | copy-start | bytes 3145732
  7.4 3.0 copy-start.2
  7.4 3.0 copy-start.12
  7.4 3.0 copy-start.10
  7.4 235.8 %all-reduce.34.cloned.1.call-start = ((), (), s32[]{:S(2)}) async-start(), calls=%async_computation.1 | async-start | bytes 2097152 | tf_op jit(solution)/shard_map/psum | solution.py:92
  11.7 156.5 %copy-start.4 = (bf16[128,1024]{1,0:T(8,128)(2,1)S(1)}, bf16[128,1024]{1,0:T(8,128)(2,1)}, u32[]{:S(2)}) copy-start(bf16[128,1024]{1,0:T(8,128)(2,1)} %param.24) | copy-start | bytes 786436
  12.5 157.6 %copy-start.9 = (s32[1,128]{1,0:T(1,128)S(1)}, s32[1,128]{1,0:T(1,128)}, u32[]{:S(2)}) copy-start(s32[1,128]{1,0:T(1,128)} %param.25) | copy-start | bytes 1540
  169.5 137.2 %all-gather.10.cloned.1.call-start = ((), (), s32[]{:S(2)}) async-start(), calls=%async_computation.2 | async-start | bytes 1064960 | tf_op jit(solution)/shard_map/all_gather | solution.py:102
  170.1 167.0 %all-gather.12.cloned.1.call-start = ((), (), s32[]{:S(2)}) async-start(), calls=%async_computation.3 | async-start | bytes 1179648 | tf_op jit(solution)/shard_map/all_gather | solution.py:106
  170.2 136.5 %copy-start.8 = (f32[512]{0:T(512)S(1)}, f32[512]{0:T(512)}, u32[]{:S(2)}) copy-start(f32[512]{0:T(512)} %param.28) | copy-start | bytes 6148
  244.6 94.2 %copy-start.1 = (bf16[256,1024]{1,0:T(8,128)(2,1)}, bf16[256,1024]{1,0:T(8,128)(2,1)S(1)}, u32[]{:S(2)}) copy-start(bf16[256,1024]{1,0:T(8,128)(2,1)S(1)} %fusion.35) | copy-start | bytes 1572868
  244.6 234.3 %copy-start.11 = (f32[4096]{0:T(1024)S(1)}, f32[4096]{0:T(1024)}, u32[]{:S(2)}) copy-start(f32[4096]{0:T(1024)} %param.29) | copy-start | bytes 49156
  309.0 170.0 %all-gather.20.cloned.1.call-start = ((), (), s32[]{:S(2)}) async-start(), calls=%async_computation.7 | async-start | bytes 1064960 | tf_op jit(solution)/shard_map/all_gather | solution.py:121
  309.7 308.0 %all-gather.14.cloned.1.call-start = ((), (), s32[]{:S(2)}) async-start(), calls=%async_computation.4 | async-start | bytes 1064960 | tf_op jit(solution)/shard_map/all_gather | solution.py:116
  310.3 452.0 %all-gather.18.cloned.1.call-start = ((), (), s32[]{:S(2)}) async-start(), calls=%async_computation.6 | async-start | bytes 4259840 | tf_op jit(solution)/shard_map/all_gather | solution.py:111
  310.9 590.4 %all-gather.22.cloned.1.call-start = ((), (), s32[]{:S(2)}) async-start(), calls=%async_computation.8 | async-start | bytes 2129920 | tf_op jit(solution)/shard_map/all_gather | solution.py:170
  337.1 280.6 %copy-start.3 = (bf16[128,4096]{1,0:T(8,128)(2,1)S(1)}, bf16[128,4096]{1,0:T(8,128)(2,1)}, u32[]{:S(2)}) copy-start(bf16[128,4096]{1,0:T(8,128)(2,1)} %all-gather.12.cloned.1.call-done) | copy-start | bytes 3145732
  338.8 281.4 %copy-start.5 = (s32[64]{0:T(128)S(1)}, s32[64]{0:T(128)}, u32[]{:S(2)}) copy-start(s32[64]{0:T(128)} %param.26) | copy-start | bytes 772
  481.6 559.6 %all-gather.16.cloned.1.call-start = ((), (), s32[]{:S(2)}) async-start(), calls=%async_computation.5 | async-start | bytes 2129920 | tf_op jit(solution)/shard_map/all_gather | solution.py:169
  620.1 508.4 %reduce-scatter.4.cloned.1.call-start = ((), (), s32[]{:S(2)}) async-start(), calls=%async_computation.9 | async-start | bytes 294912
  1045.6 1.9 copy-start.6
  1051.8 1.9 copy-start.6
  1058.1 1.9 copy-start.6
  1064.3 1.9 copy-start.6
  1070.6 1.9 copy-start.6
  1076.8 1.9 copy-start.6
  1083.1 1.9 copy-start.6
  1089.3 1.9 copy-start.6
  1091.2 1.4 copy-start.7
Sparse Core Ops, SparseCore 0:
  169.7 73.5 all-reduce.33
  309.1 27.9 all-gather.11
  340.1 138.8 all-gather.19
  481.7 135.9 all-gather.13
  620.5 141.6 all-gather.17
  765.0 136.1 all-gather.21
  904.2 137.0 all-gather.15
  1092.8 35.7 reduce-scatter.3
Sparse Core Ops, SparseCore 1:
  173.0 133.7 all-gather.9
where the time goes:
time: 1140 us
  waiting for transfers between devices  888 us (78%)
  blocking collectives  153 us (13%)
  matrix products  41.2 us (4%)
  other arithmetic  27.3 us (2%)
  between operations  15.9 us (1%)
  local copies, waits for them, and re-layouts  11.6 us (1%)
    all_gather x2, blocking collectives, prefix(): pieces = jax.tree.map(lambda part: lax.all_gather(part, axis), value)  153 us
    all_gather x1, waiting for transfers between devices, on_device(): lax.all_gather(value_weight, 'seq', axis=0, tiled=True)  140 us
    all_gather x1, waiting for transfers between devices, on_device(): key_piece = lax.all_gather(key_rows, 'seq', axis=0, tiled=True)  140 us
    all_gather x1, waiting for transfers between devices, on_device(): lax.all_gather(query_weight, 'seq', axis=0, tiled=True)  137 us
    all_gather x1, waiting for transfers between devices, on_device(): lax.all_gather(key_weight, 'seq', axis=0, tiled=True)  136 us
    all_gather x1, waiting for transfers between devices, on_device(): value_piece = lax.all_gather(value_rows, 'seq', axis=0, tiled=True)  136 us
    psum x1, waiting for transfers between devices, on_device(): mixed_sum = lax.psum(partial_value, 'mp')  73 us
    all_gather x1, waiting for transfers between devices, on_device(): lax.all_gather(up_weight, 'seq', axis=0, tiled=True)  61.3 us
  transfers between devices with their start and end apart: 9, of which 9 were waited for; matrix products, arithmetic and copies ran while one was open for 1% of the time, Pallas kernels for 0%

commit v1 on v0

--- a/solution.py
+++ b/solution.py
@@ -10,6 +10,13 @@
 eps = 1e-05
 masked = -1e30
 far_index = 1073741824
+
+
+def gather_over(value, axis, dim):
+    size = lax.axis_size(axis)
+    pieces = jnp.stack([value for _ in range(size)])
+    pieces = lax.all_to_all(pieces, axis, split_axis=0, concat_axis=0)
+    return jnp.concatenate(pieces, axis=dim)
 
 
 def prefix(value, axis, join, neutral):
@@ -112,9 +119,7 @@
         preferred_element_type=jnp.float32,
     )
     key_part = jnp.dot(
-        columns,
-        lax.all_gather(key_weight, "seq", axis=0, tiled=True),
-        preferred_element_type=jnp.float32,
+        columns, gather_over(key_weight, "seq", 0), preferred_element_type=jnp.float32
     )
     value_part = jnp.dot(
         columns,

time: 1140 us -> 1000 us (0.88)
  waiting for transfers between devices: 888 us -> 737 us
  starting transfers between devices: 0.36 us -> 11.8 us
    all_gather x1 -> x0, waiting for transfers between devices: 136 us -> none  [on_device(): lax.all_gather(key_weight, 'seq', axis=0, tiled=True)]
    all_gather x1, waiting for transfers between devices: 26.2 us -> 13.9 us  [on_device(): widened = lax.all_gather(widened_share, 'mp', axis=1, tiled=True)]
    all_to_all x0 -> x1, starting transfers between devices: none -> 11.5 us  [gather_over(): pieces = lax.all_to_all(pieces, axis, split_axis=0, concat_axis=0)]
    unnamed x10 -> x9, waiting for transfers between devices: 38.2 us -> 37.6 us
  transfers between devices with their start and end apart: 9 -> 9, of which waited for: 9 -> 8; matrix products, arithmetic and copies ran while one was open for 1% -> 2% of each run, Pallas kernels for 0% -> 0%
where the time goes in v1:
time: 1000 us
  waiting for transfers between devices  737 us (74%)
  blocking collectives  153 us (15%)
  matrix products  40 us (4%)
  other arithmetic  27.3 us (3%)
  between operations  15.9 us (2%)
  local copies, waits for them, and re-layouts  12.9 us (1%)
  starting transfers between devices  11.8 us (1%)
    all_gather x2, blocking collectives, prefix(): pieces = jax.tree.map(lambda part: lax.all_gather(part, axis), value)  153 us
    all_gather x1, waiting for transfers between devices, on_device(): lax.all_gather(value_weight, 'seq', axis=0, tiled=True)  140 us
    all_gather x1, waiting for transfers between devices, on_device(): key_piece = lax.all_gather(key_rows, 'seq', axis=0, tiled=True)  140 us
    all_gather x1, waiting for transfers between devices, on_device(): value_piece = lax.all_gather(value_rows, 'seq', axis=0, tiled=True)  136 us
    all_gather x1, waiting for transfers between devices, on_device(): lax.all_gather(query_weight, 'seq', axis=0, tiled=True)  136 us
    psum x1, waiting for transfers between devices, on_device(): mixed_sum = lax.psum(partial_value, 'mp')  73 us
    all_gather x1, waiting for transfers between devices, on_device(): lax.all_gather(up_weight, 'seq', axis=0, tiled=True)  61.3 us
    unnamed x9, waiting for transfers between devices  37.6 us
  transfers between devices with their start and end apart: 9, of which 8 were waited for; matrix products, arithmetic and copies ran while one was open for 2% of the time, Pallas kernels for 0%

profile of v1, /device:TPU:8, one launch (start us, length us, event | category | flops | bytes accessed | tf_op | source)
XLA Modules:
  0.0 1000.2 jit_solution(7926342078974162280)
XLA Ops:
  8.8 1.5 negate_exponential_fusion
  12.6 79.6 %all-gather.1 = f32[64,1,128]{2,1,0:T(1,128)S(1)} all-gather(f32[1,1,128]{2,1,0:T(1,128)S(1)} %add_bitcast_fusion), channel_id=1, replica_groups=mesh['seq'=64,'mp'=8] {'seq'}, dimensions={0}, use_global_device_ids=true | all-gather | bytes 33280 | tf_op jit(solution)/shard_map/all_gather | solution.py:24
  92.3 73.3 %all-gather = f32[64,1,128]{2,1,0:T(1,128)S(1)} all-gather(f32[1,1,128]{2,1,0:T(1,128)S(1)} %add_bitcast_fusion.1), channel_id=1, replica_groups=mesh['seq'=64,'mp'=8] {'seq'}, dimensions={0}, use_global_device_ids=true | all-gather | bytes 33280 | tf_op jit(solution)/shard_map/all_gather | solution.py:24
  165.6 2.6 while.34
  170.2 73.0 %all-reduce.34.cloned.1.call-done = f32[256,1024]{1,0:T(8,128)} async-done(((f32[256,1024]{1,0:T(8,128)}), f32[256,1024]{1,0:T(8,128)}) %all-reduce.34.cloned.1.call-update) | async-done | bytes 1048592 | tf_op jit(solution)/shard_map/psum | solution.py:99
  245.5 61.3 %all-gather.9.cloned.1.call-done = bf16[1024,512]{1,0:T(8,128)(2,1)} async-done(((bf16[16,512]{1,0:T(8,128)(2,1)}), bf16[1024,512]{1,0:T(8,128)(2,1)}) %all-gather.9.cloned.1.call-update) | async-done | bytes 1048592 | tf_op jit(solution)/shard_map/all_gather | solution.py:109
  306.7 2.2 fusion.31
  311.6 11.5 %all-to-all-start = ((bf16[64,64,128]{2,1,0:T(8,128)(2,1)}), bf16[64,64,128]{2,1,0:T(8,128)(2,1)S(1)}, u32[]{:S(2)}, u32[]{:S(2)}) async-start(bf16[64,64,128]{2,1,0:T(8,128)(2,1)} %stack.2), calls=%async_computation | async-start | bytes 2097152 | tf_op jit(solution)/shard_map/all_to_all | solution.py:18
  323.2 13.9 %all-gather.11.cloned.1.call-done = bf16[128,4096]{1,0:T(8,128)(2,1)} async-done(((bf16[128,512]{1,0:T(8,128)(2,1)}), bf16[128,4096]{1,0:T(8,128)(2,1)}) %all-gather.11.cloned.1.call-update) | async-done | bytes 1048592 | tf_op jit(solution)/shard_map/all_gather | solution.py:113
  337.1 1.6 fusion.28
  338.8 140.2 %all-gather.17.cloned.1.call-done = bf16[4096,128]{1,0:T(8,128)(2,1)} async-done(((bf16[64,128]{1,0:T(8,128)(2,1)}), bf16[4096,128]{1,0:T(8,128)(2,1)}) %all-gather.17.cloned.1.call-update) | async-done | bytes 1048592 | tf_op jit(solution)/shard_map/all_gather | solution.py:126
  478.9 2.7 convolution_convert_fusion.2
  485.2 1.9 add_select_fusion.3
  487.8 135.6 %all-gather.15.cloned.1.call-done = bf16[4096,512]{1,0:T(8,128)(2,1)} async-done(((bf16[64,512]{1,0:T(8,128)(2,1)}), bf16[4096,512]{1,0:T(8,128)(2,1)}) %all-gather.15.cloned.1.call-update) | async-done | bytes 4194320 | tf_op jit(solution)/shard_map/all_gather | solution.py:118
  623.5 2.9 convolution_convert_fusion.1
  626.5 135.9 %all-gather.19.cloned.1.call-done = bf16[8192,128]{1,0:T(8,128)(2,1)} async-done(((bf16[128,128]{1,0:T(8,128)(2,1)}), bf16[8192,128]{1,0:T(8,128)(2,1)}) %all-gather.19.cloned.1.call-update) | async-done | bytes 2097168 | tf_op jit(solution)/shard_map/all_gather | solution.py:175
  762.4 139.9 %all-gather.13.cloned.1.call-done = bf16[8192,128]{1,0:T(8,128)(2,1)} async-done(((bf16[128,128]{1,0:T(8,128)(2,1)}), bf16[8192,128]{1,0:T(8,128)(2,1)}) %all-gather.13.cloned.1.call-update) | async-done | bytes 2097168 | tf_op jit(solution)/shard_map/all_gather | solution.py:174
  902.3 50.0 %while.35 = (s32[]{:T(128)}, f32[1,512]{1,0:T(1,128)S(1)}, f32[1,512]{1,0:T(1,128)S(1)}, f32[1,512,128]{2,1,0:T(8,128)S(1)}, s32[64]{0:T(128)S(1)}, /*index=5*/s...) while((s32[]{:T(128)}, f32[1,512]{1,0:T(1,128)S(1)}, ...), condition=%wide.region_13.14_spmd.clone, body=%wide.region_8.13_spmd.clone.sunk | while | flops 273186304 | bytes 7548097 | solution.py:188
  904.0 2.0 fusion.78
  910.2 2.0 fusion.78
  913.3 1.5 fusion.82
  916.5 2.0 fusion.78
  919.5 1.5 fusion.82
  922.7 2.0 fusion.78
  925.8 1.5 fusion.82
  929.0 2.0 fusion.78
  935.2 2.0 fusion.78
  941.5 2.0 fusion.78
  947.7 2.0 fusion.78
  950.8 1.5 fusion.82
  953.7 35.8 %reduce-scatter.4.cloned.1.call-done = bf16[128,128]{1,0:T(8,128)(2,1)} async-done(((bf16[1024,128]{1,0:T(8,128)(2,1)}), bf16[128,128]{1,0:T(8,128)(2,1)}) %reduce-scatter.4.cloned.1.call-update) | async-done | bytes 32784
  991.3 1.5 add_convert_fusion
  (353 shorter events, 46.2 us)
Async XLA Ops:
  7.4 945.1 %copy-start = (bf16[512,1024]{1,0:T(8,128)(2,1)S(1)}, bf16[512,1024]{1,0:T(8,128)(2,1)}, u32[]{:S(2)}) copy-start(bf16[512,1024]{1,0:T(8,128)(2,1)} %param.33) | copy-start | bytes 3145732
  7.4 3.0 copy-start.2
  7.4 3.0 copy-start.13
  7.4 3.0 copy-start.11
  7.4 235.8 %all-reduce.34.cloned.1.call-start = ((), (), s32[]{:S(2)}) async-start(), calls=%async_computation.2 | async-start | bytes 2097152 | tf_op jit(solution)/shard_map/psum | solution.py:99
  11.7 156.5 %copy-start.4 = (bf16[128,1024]{1,0:T(8,128)(2,1)S(1)}, bf16[128,1024]{1,0:T(8,128)(2,1)}, u32[]{:S(2)}) copy-start(bf16[128,1024]{1,0:T(8,128)(2,1)} %param.24) | copy-start | bytes 786436
  12.5 157.6 %copy-start.10 = (s32[1,128]{1,0:T(1,128)S(1)}, s32[1,128]{1,0:T(1,128)}, u32[]{:S(2)}) copy-start(s32[1,128]{1,0:T(1,128)} %param.25) | copy-start | bytes 1540
  169.5 137.2 %all-gather.9.cloned.1.call-start = ((), (), s32[]{:S(2)}) async-start(), calls=%async_computation.3 | async-start | bytes 1064960 | tf_op jit(solution)/shard_map/all_gather | solution.py:109
  170.1 167.0 %all-gather.11.cloned.1.call-start = ((), (), s32[]{:S(2)}) async-start(), calls=%async_computation.4 | async-start | bytes 1179648 | tf_op jit(solution)/shard_map/all_gather | solution.py:113
  170.2 136.5 %copy-start.9 = (f32[512]{0:T(512)S(1)}, f32[512]{0:T(512)}, u32[]{:S(2)}) copy-start(f32[512]{0:T(512)} %param.28) | copy-start | bytes 6148
  244.6 67.0 %copy-start.1 = (bf16[256,1024]{1,0:T(8,128)(2,1)}, bf16[256,1024]{1,0:T(8,128)(2,1)S(1)}, u32[]{:S(2)}) copy-start(bf16[256,1024]{1,0:T(8,128)(2,1)S(1)} %fusion.35) | copy-start | bytes 1572868
  244.6 65.7 %copy-start.7 = (bf16[64,128]{1,0:T(8,128)(2,1)S(1)}, bf16[64,128]{1,0:T(8,128)(2,1)}, u32[]{:S(2)}) copy-start(bf16[64,128]{1,0:T(8,128)(2,1)} %param.31) | copy-start | bytes 49156
  309.0 170.0 %all-gather.17.cloned.1.call-start = ((), (), s32[]{:S(2)}) async-start(), calls=%async_computation.7 | async-start | bytes 1064960 | tf_op jit(solution)/shard_map/all_gather | solution.py:126
  309.7 313.8 %all-gather.15.cloned.1.call-start = ((), (), s32[]{:S(2)}) async-start(), calls=%async_computation.6 | async-start | bytes 4259840 | tf_op jit(solution)/shard_map/all_gather | solution.py:118
  310.3 168.7 %copy-start.12 = (f32[4096]{0:T(1024)S(1)}, f32[4096]{0:T(1024)}, u32[]{:S(2)}) copy-start(f32[4096]{0:T(1024)} %param.29) | copy-start | bytes 49156
  311.6 170.1 %all-to-all-start = ((bf16[64,64,128]{2,1,0:T(8,128)(2,1)}), bf16[64,64,128]{2,1,0:T(8,128)(2,1)S(1)}, u32[]{:S(2)}, u32[]{:S(2)}) async-start(bf16[64,64,128]{2,1,0:T(8,128)(2,1)} %stack.2), calls=%async_computation | async-start | bytes 2097152 | tf_op jit(solution)/shard_map/all_to_all | solution.py:18
  323.1 439.3 %all-gather.19.cloned.1.call-start = ((), (), s32[]{:S(2)}) async-start(), calls=%async_computation.8 | async-start | bytes 2129920 | tf_op jit(solution)/shard_map/all_gather | solution.py:175
  337.1 144.6 %copy-start.3 = (bf16[128,4096]{1,0:T(8,128)(2,1)S(1)}, bf16[128,4096]{1,0:T(8,128)(2,1)}, u32[]{:S(2)}) copy-start(bf16[128,4096]{1,0:T(8,128)(2,1)} %all-gather.11.cloned.1.call-done) | copy-start | bytes 3145732
  338.7 144.2 %copy-start.5 = (s32[64]{0:T(128)S(1)}, s32[64]{0:T(128)}, u32[]{:S(2)}) copy-start(s32[64]{0:T(128)} %param.26) | copy-start | bytes 772
  481.6 420.7 %all-gather.13.cloned.1.call-start = ((), (), s32[]{:S(2)}) async-start(), calls=%async_computation.5 | async-start | bytes 2129920 | tf_op jit(solution)/shard_map/all_gather | solution.py:174
  482.8 506.7 %reduce-scatter.4.cloned.1.call-start = ((), (), s32[]{:S(2)}) async-start(), calls=%async_computation.9 | async-start | bytes 294912
  906.7 1.9 copy-start.6
  912.9 1.9 copy-start.6
  919.2 1.9 copy-start.6
  925.4 1.9 copy-start.6
  931.6 1.9 copy-start.6
  937.9 1.9 copy-start.6
  944.1 1.9 copy-start.6
  950.4 1.9 copy-start.6
  952.3 1.4 copy-start.8
Sparse Core Ops, SparseCore 0:
  169.7 73.5 all-reduce.33
  309.1 28.0 all-gather.10
  340.1 138.8 all-gather.16
  481.7 141.6 all-gather.14
  626.2 136.1 all-gather.18
  765.2 137.0 all-gather.12
  953.8 35.6 reduce-scatter.3
Sparse Core Ops, SparseCore 1:
  173.0 133.7 all-gather.8
